TPU v7x, 32 devices: a whole 2x2x4 slice. The times are simulated.
32 devices in a mesh: slab: 2 (over x), clus: 16 (over z, y, core).
Axes of the slice: x: 2, y: 2, z: 4, core: 2. Of those that a mesh axis runs over, the one named last changes fastest.
Arguments:
- emb: bfloat16 [8192, 1024], P(('slab', 'clus')), parts along dimension 0, may hold values from -4000 to 4000
- wanted: int32 [512], P(('slab', 'clus')), parts along dimension 0, may hold values from 0 to 31, as said below
- counts: int32 [64], P('slab'), parts along dimension 0, may hold values from 2 to 128, as said below
Outputs:
- best: float32 [16, 8192], P(None, ('slab', 'clus')), parts along dimension 1
- own: float32 [8192], P(('slab', 'clus')), parts along dimension 0
There are 2 independent parts, one for each index of `slab`. A program takes and returns all parts, laid end to end along the dimension named above; each array names one. Nothing has to cross between parts.
Inputs may be any that keep to these rules, and one draw needn't show every extreme that they name: `wanted`: the 16 entries of one group name exactly one cluster of every group (group = cluster // 2), one entry per group. `counts`: some cluster has exactly 128 live rows.
All inputs are finite; a program needn't handle non-finite values.
Results may differ from a plain program's by a relative error of at most 0.0015.
Values may be sent and summed in bfloat16 or wider, within the bound.
A program may use at most 128 MiB of HBM per device.

v0:
```python
import jax
import jax.numpy as jnp
from jax import lax
from jax.sharding import PartitionSpec as P

TILE = 128


def unit_rows(values):
    wide = values.astype(jnp.float32)
    total = jnp.sum(wide * wide, axis=-1, keepdims=True)
    return (wide * lax.rsqrt(total + 1e-06)).astype(jnp.bfloat16)


def body(emb, wanted, counts):
    rows_dev, width = emb.shape
    req_count = wanted.shape[0]
    clus_dev = rows_dev // TILE
    peers = lax.axis_size("clus")
    mine = lax.axis_index("clus")
    capacity = req_count // peers
    unit = unit_rows(emb)
    owners = wanted // clus_dev
    local_ids = wanted % clus_dev
    positions = jnp.arange(req_count)
    earlier = positions[None, :] < positions[:, None]
    slots = jnp.sum((owners[:, None] == owners[None, :]) & earlier, axis=1)
    slot_ids = jnp.arange(capacity)[None, :, None]
    peer_ids = jnp.arange(peers)[:, None, None]
    marks = (owners[None, None, :] == peer_ids) & (slots[None, None, :] == slot_ids)
    request = jnp.sum(jnp.where(marks, local_ids[None, None, :] + 1, 0), axis=2) - 1
    asked = lax.all_to_all(request, "clus", split_axis=0, concat_axis=0, tiled=True)
    picks = jnp.clip(asked, 0, clus_dev - 1).reshape(-1)
    own_counts = lax.dynamic_slice_in_dim(counts, mine * clus_dev, clus_dev)
    pick_counts = jnp.sum(
        jnp.where(jnp.arange(clus_dev)[None, :] == picks[:, None], own_counts[None, :], 0), axis=1
    )
    index = jnp.arange(TILE)
    blocks = unit.reshape(clus_dev, TILE, width)
    outgoing = jnp.take(blocks, picks, axis=0)
    row_used = (index[None, :] < pick_counts[:, None])[:, :, None]
    outgoing = jnp.where(row_used, outgoing, outgoing[:, :1, :])
    outgoing = outgoing.reshape(peers, capacity, TILE, width)
    arrived = lax.all_to_all(outgoing, "clus", split_axis=0, concat_axis=0, tiled=True)
    items = arrived.shape[1]
    grouped = arrived.reshape(peers // 8, 8 * items * TILE, width)

    def score_block(tile_block):
        product = jnp.dot(unit, tile_block.T, preferred_element_type=jnp.float32)
        return jnp.max(product.reshape(rows_dev, 8 * items, TILE), axis=2).T

    scored = lax.map(score_block, grouped)
    scores = scored.reshape(peers, items, rows_dev)
    wanted_rows = owners * capacity + slots
    best = jnp.take(scores.reshape(peers * capacity, rows_dev), wanted_rows, axis=0)
    row_live = (index[None, :] < own_counts[:, None]).reshape(rows_dev)
    best = jnp.where(row_live[None, :], best, 0.0)
    inner = jnp.einsum("bid,bjd->bij", blocks, blocks, preferred_element_type=jnp.float32)
    keep = (index[None, None, :] < own_counts[:, None, None]) & (index[:, None] != index[None, :])[
        None
    ]
    own = jnp.max(jnp.where(keep, inner, -jnp.inf), axis=2).reshape(rows_dev)
    own = jnp.where(row_live, own, 0.0)
    return (best, own)


def solution(mesh):
    in_specs = (P(("slab", "clus"), None), P(("slab", "clus")), P("slab"))
    out_specs = (P(None, ("slab", "clus")), P(("slab", "clus")))
    return jax.shard_map(body, mesh=mesh, in_specs=in_specs, out_specs=out_specs, check_vma=False)
```

profile of v0, /device:TPU:13, one launch (start us, length us, event | category | flops | bytes accessed | tf_op | source)
XLA Modules:
  0.0 126.4 jit_solution(7305811616904637816)
XLA Ops:
  0.6 0.7 and_select_fusion.1
  1.3 0.2 convert_reduce_fusion
  1.5 0.1 select_reduce_fusion
  1.6 0.7 copy.9
  2.3 6.5 %all-to-all-start = ((s32[16,1,1]{2,1,0:T(1,128)}), s32[16,1,1]{2,1,0:T(1,128)S(1)}, u32[]{:S(2)}, u32[]{:S(2)}) async-start(s32[16,1,1]{2,1,0:T(1,128)} %copy.9), calls=%async_computation | async-start | bytes 16384 | tf_op jit(solution)/shard_map/all_to_all | solution.py:32
  8.8 1.2 fusion.9
  10.1 1.2 fusion.10
  11.3 0.7 dynamic_slice.7
  12.0 0.6 all-to-all-done
  12.6 0.4 clamp_reduce_fusion
  13.0 2.8 %gather_fusion = bf16[16,128,1024]{2,1,0:T(8,128)(2,1)} fusion(bf16[2,128,1024]{2,1,0:T(8,128)(2,1)S(1)} %bitcast.49, s32[1024]{0:T(1024)S(1)} %pad_clamp_fusion.1), kind=kCustom, calls=%fused_computation | custom fusion | bytes 8388672 | tf_op jit(solution)/shard_map/jit(_take)/gather | solution.py:40
  15.8 1.1 broadcast_select_fusion
  16.9 0.1 fusion.13
  17.0 0.1 iota_compare_fusion.2
  17.1 3.9 %fusion.7 = bf16[16,1,128,1024]{3,2,1,0:T(8,128)(2,1)} fusion(bf16[16,128,1024]{2,1,0:T(8,128)(2,1)} %gather_fusion, pred[16]{0:T(512)(128)(4,1)S(1)} %compare_and_fusion, pred[16,128]{1,0:T(8,128)(4,1)S(1)} %iota_compare_fusion.2, bf16[16,1024]{1,0:T(8,128)(2,1)S(1)} %bitcast.52), kind=kLoop, calls=%fused_computation.10 | loop fusion | flops 4194304 | bytes 8423440 | tf_op jit(solution)/shard_map/jit(_where)/select_n | solution.py:42
  20.9 7.0 %all-to-all-start.1 = ((bf16[16,1,128,1024]{3,2,1,0:T(8,128)(2,1)}), bf16[16,1,128,1024]{3,2,1,0:T(8,128)(2,1)}, u32[]{:S(2)}, u32[]{:S(2)}) async-start(bf16[16,1,128,1024]{3,2,1,0:T(8,128)(2,1)} %fusion.7), calls=%async_computation.1 | async-start | bytes 8388608 | tf_op jit(solution)/shard_map/all_to_all | solution.py:44
  27.9 0.1 iota_compare_fusion.4
  28.0 0.3 fusion.8
  28.3 0.6 bitcast_select_fusion.1
  29.0 91.4 %all-to-all-done.1 = bf16[16,1,128,1024]{3,2,1,0:T(8,128)(2,1)} async-done(((bf16[16,1,128,1024]{3,2,1,0:T(8,128)(2,1)}), bf16[16,1,128,1024]{3,2,1,0:T(8,128)(2,1)}, u32[]{:S(2)}, u32[]{:S(2)}) %all-to-all-start.1) | async-done | bytes 4194336 | tf_op jit(solution)/shard_map/all_to_all | solution.py:44
  120.4 4.7 %while.10 = (s32[]{:T(128)}, f32[2,8,256]{2,1,0:T(8,128)S(1)}, bf16[2,1024,1024]{2,1,0:T(8,128)(2,1)}, bf16[256,1024]{1,0:T(8,128)(2,1)S(1)}, s32[]{:T(128)}) while((s32[]{:T(128)}, f32[2,8,256]{2,1,0:T(8,128)S(1)}, bf16[2,1024,1024]{2,1,0:T(8,128)(2,1)}, bf16[256,1024]{1,0:T(8,128)(2,1)S(1)}, s32[]{:T(128)}) %tuple.26), condition=%wide.region_6.7_spmd, body=%wide.region_4.6_spmd.sunk | while | flops 537131008 | bytes 2646593 | solution.py:52
  120.4 2.3 %bitcast_reduce_fusion.2 = f32[256,8]{0,1:T(8,128)S(1)} fusion(bf16[256,1024]{1,0:T(8,128)(2,1)S(1)} %get-tuple-element.78, bf16[2,1024,1024]{2,1,0:T(8,128)(2,1)} %get-tuple-element.77, s32[]{:T(128)} %get-tuple-element.70), kind=kOutput, calls=%fused_computation.5.clone.1 | convolution fusion | flops 537131008 | bytes 2630144 | tf_op jit(solution)/shard_map/while/body/eval_jaxpr/dot_general | solution.py:49
  122.8 2.3 %bitcast_reduce_fusion.2 = f32[256,8]{0,1:T(8,128)S(1)} fusion(bf16[256,1024]{1,0:T(8,128)(2,1)S(1)} %get-tuple-element.78, bf16[2,1024,1024]{2,1,0:T(8,128)(2,1)} %get-tuple-element.77, s32[]{:T(128)} %get-tuple-element.70), kind=kOutput, calls=%fused_computation.5.clone.1 | convolution fusion | flops 537131008 | bytes 2630144 | tf_op jit(solution)/shard_map/while/body/eval_jaxpr/dot_general | solution.py:49
  125.1 0.6 gather_fusion.1
  125.7 0.7 select_select_fusion
  (12 shorter events, 0.1 us)
Async XLA Ops:
  2.3 10.3 %all-to-all-start = ((s32[16,1,1]{2,1,0:T(1,128)}), s32[16,1,1]{2,1,0:T(1,128)S(1)}, u32[]{:S(2)}, u32[]{:S(2)}) async-start(s32[16,1,1]{2,1,0:T(1,128)} %copy.9), calls=%async_computation | async-start | bytes 16384 | tf_op jit(solution)/shard_map/all_to_all | solution.py:32
  20.9 99.5 %all-to-all-start.1 = ((bf16[16,1,128,1024]{3,2,1,0:T(8,128)(2,1)}), bf16[16,1,128,1024]{3,2,1,0:T(8,128)(2,1)}, u32[]{:S(2)}, u32[]{:S(2)}) async-start(bf16[16,1,128,1024]{3,2,1,0:T(8,128)(2,1)} %fusion.7), calls=%async_computation.1 | async-start | bytes 8388608 | tf_op jit(solution)/shard_map/all_to_all | solution.py:44
where the time goes:
time: 127 us; the launch traced here: 126 us
  waiting for transfers between devices  92 us (72%)
  starting transfers between devices  13.5 us (11%)
  other arithmetic  10.3 us (8%)
  matrix products  5 us (4%)
  local copies, waits for them, and re-layouts  4.81 us (4%)
    all_to_all x1, waiting for transfers between devices, body(): lax.all_to_all(outgoing, 'clus', split_axis=0, concat_axis=0, tiled=True)  91.4 us
    all_to_all x1, starting transfers between devices, body(): lax.all_to_all(outgoing, 'clus', split_axis=0, concat_axis=0, tiled=True)  6.97 us
    all_to_all x1, starting transfers between devices, body(): lax.all_to_all(request, 'clus', split_axis=0, concat_axis=0, tiled=True)  6.52 us
    dot_general x2, matrix products, score_block(): product = jnp.dot(unit, tile_block.T, preferred_element_type=jnp.float32)  4.69 us
    select_n x1, other arithmetic, body(): outgoing = jnp.where(row_used, outgoing, outgoing[:, :1, :])  3.86 us
    gather x1, local copies, waits for them, and re-layouts, body(): outgoing = jnp.take(blocks, picks, axis=0)  2.79 us
  transfers between devices with their start and end apart: 2, of which 2 were waited for; matrix products, arithmetic and copies ran while one was open for 3% of the time, Pallas kernels for 0%

commit v1 on v0

v1 whole, which is shorter than its diff:
```python
import functools
import jax
import jax.numpy as jnp
from jax import lax
from jax.experimental import pallas as pl
from jax.experimental.pallas import tpu as pltpu
from jax.sharding import PartitionSpec as P

TILE = 128
CORES = 2
LAYER = 4
MESH = pl.DeviceIdType.MESH
NT = (((1,), (1,)), ((), ()))


def ring(chips, cols):
    def chip_at(pos):
        pos = lax.rem(pos + 4 * chips, chips)
        if cols == 1:
            return pos
        back = pos // (chips // 2)
        return (pos + back * (chips - 1 - 2 * pos)) * 2 + back

    def pos_of(chip):
        if cols == 1:
            return chip
        z, y = chip // 2, lax.rem(chip, 2)
        return z + y * (chips - 1 - 2 * z)

    return chip_at, pos_of


def kernel(
    chips, cols, wanted_ref, counts_ref, emb_ref, best_ref, own_ref,
    unit, from_l, from_r, across, table, res_a, res_b,
    r_send, r_recv, l_send, l_recv, x_send, x_recv,
    a_send, a_recv, b_send, b_recv,
):
    rows, width = emb_ref.shape
    parts = rows // TILE
    reach = chips // 4
    far = 2 * reach
    chip_at, pos_of = ring(chips, cols)
    me = lax.axis_index("clus")
    core = lax.rem(me, CORES)
    other = 1 - core
    pos = pos_of(me // CORES)

    def dev(p, c):
        return chip_at(p) * CORES + c

    def crossed(p):
        return lax.rem(p + 4 * chips, chips) // (chips // 2)

    def swap(p, c):
        x = crossed(p)
        return c + x * (1 - 2 * c)

    barrier = pltpu.get_barrier_semaphore()

    def greet(target):
        pl.semaphore_signal(barrier, inc=1, device_id={"clus": target}, device_id_type=MESH)

    greet(dev(pos, other))
    for i in range(1, reach + 1):
        greet(dev(pos + i, core))
    for j in range(1, reach):
        greet(dev(pos - j, 0))
        greet(dev(pos - j, 1))
    greet(dev(pos - reach, swap(pos - reach, core)))

    @pl.when(crossed(pos) == 1)
    def _():
        greet(dev(pos + 1, other))

    def remote(src, dst, send, recv, target):
        return pltpu.make_async_remote_copy(
            src_ref=src, dst_ref=dst, send_sem=send, recv_sem=recv,
            device_id={"clus": target}, device_id_type=MESH,
        )

    def right(h, q):
        src = unit if h == 0 else from_l.at[h - 1]
        return remote(src.at[q], from_l.at[h, q], r_send.at[h, q], r_recv.at[h, q], dev(pos + 1, core))

    def left(h, q):
        src = unit if h == 0 else from_r.at[h - 1]
        c = swap(pos - 1, core) if h == reach - 1 else core
        return remote(src.at[q], from_r.at[h, q], l_send.at[h, q], l_recv.at[h, q], dev(pos - 1, c))

    def cross(h, q):
        src = unit if h == 0 else from_r.at[h - 1]
        return remote(src.at[q], across.at[h, q], x_send.at[h, q], x_recv.at[h, q], dev(pos, other))

    def normalize(q):
        step = 32
        for s in range(0, TILE, step):
            wide = emb_ref[q * TILE + s : q * TILE + s + step, :].astype(jnp.float32)
            total = jnp.sum(wide * wide, axis=1, keepdims=True)
            unit[q, s : s + step, :] = (wide * lax.rsqrt(total + 1e-06)).astype(jnp.bfloat16)

    for q in range(parts):
        normalize(q)
        if q == 0:
            pl.semaphore_wait(barrier, 3 * reach + crossed(pos - 1))
        right(0, q).start()
        left(0, q).start()
        cross(0, q).start()

    def rows_of(ref, q):
        return ref[q]

    def product(x, y):
        return lax.dot_general(x, y, NT, preferred_element_type=jnp.float32)

    def top(prod, cluster):
        index = lax.broadcasted_iota(jnp.int32, prod.shape, 0)
        live = index < counts_ref[cluster]
        return jnp.max(jnp.where(live, prod, -jnp.inf), axis=0, keepdims=True)

    def block(ref):
        return ref[...].reshape(parts * TILE, width)

    self_prod = product(block(unit), block(unit))
    for t in range(parts):
        piece = self_prod[t * TILE : (t + 1) * TILE]
        table[me * parts + t] = top(piece, me * parts + t)
        square = piece[:, t * TILE : (t + 1) * TILE]
        i0 = lax.broadcasted_iota(jnp.int32, square.shape, 0)
        i1 = lax.broadcasted_iota(jnp.int32, square.shape, 1)
        count = counts_ref[me * parts + t]
        keep = (i0 < count) & (i0 != i1)
        value = jnp.max(jnp.where(keep, square, -jnp.inf), axis=0, keepdims=True)
        lane = lax.broadcasted_iota(jnp.int32, value.shape, 1)
        own_ref[:, t * TILE : (t + 1) * TILE] = jnp.where(lane < count, value, 0.0)

    for q in range(parts):
        cross(0, q).wait_recv()
    mate = dev(pos, other)
    mate_prod = product(block(across.at[0]), block(unit))
    for t in range(parts):
        table[mate * parts + t] = top(mate_prod[t * TILE : (t + 1) * TILE], mate * parts + t)

    def split(d):
        j = max(1, d // 2)
        return d - j, j

    def a_msg(d):
        i, j = split(d)
        if d == far:
            b = dev(pos + j, swap(pos, core))
            count = parts
        else:
            b = dev(pos + j, 0)
            count = parts * CORES
        return remote(
            res_a.at[d - 1, pl.ds(0, count)], table.at[pl.ds(b * parts, count)],
            a_send.at[d - 1], a_recv.at[d - 1], dev(pos - i, core),
        )

    def b_msg(d, e, slot):
        i, j = split(d)
        target = dev(pos + j, swap(pos, core) if d == far else e)
        a = dev(pos - i, core)
        return remote(
            res_b.at[d - 1, e], table.at[pl.ds(a * parts, parts)],
            b_send.at[d - 1, e], b_recv.at[d - 1, slot], target,
        )

    def messages(d):
        i, _ = split(d)
        found = [b_msg(d, e, 0 if d == far else core) for e in range(1 if d == far else CORES)]
        if i > 0:
            found.append(a_msg(d))
        return found

    def score(d, a_ref, b_ref, e, b_dev, a_q, b_q):
        i, _ = split(d)
        a_dev = dev(pos - i, core)
        qa, qb = a_q, b_q
        a = jnp.concatenate([a_ref[q] for q in qa], axis=0) if len(qa) > 1 else a_ref[qa[0]]
        b = jnp.concatenate([b_ref[q] for q in qb], axis=0) if len(qb) > 1 else b_ref[qb[0]]
        up = product(b, a)
        for n, t in enumerate(qb):
            value = top(up[n * TILE : (n + 1) * TILE], b_dev * parts + t)
            lanes = slice(qa[0] * TILE, (qa[-1] + 1) * TILE)
            if i == 0:
                table[b_dev * parts + t, :, lanes] = value
            else:
                slot = t if d == far else e * parts + t
                res_a[d - 1, slot, :, lanes] = value
        down = product(a, b)
        for n, t in enumerate(qa):
            value = top(down[n * TILE : (n + 1) * TILE], a_dev * parts + t)
            res_b[d - 1, 0 if d == far else e, t, :, qb[0] * TILE : (qb[-1] + 1) * TILE] = value

    every = list(range(parts))

    def near(d, a_q):
        i, j = split(d)
        a_ref = unit if i == 0 else from_l.at[i - 1]
        for mine in (True, False):
            b_ref = from_r.at[j - 1] if mine else across.at[j]
            e = core if mine else other
            score(d, a_ref, b_ref, e, dev(pos + j, e), a_q, every)

    for h in range(1, reach + 1):
        last = h == reach
        for q in range(parts):
            right(h - 1, q).wait_recv()
            if not last:
                right(h, q).start()
            left(h - 1, q).wait_recv()
            if not last:
                left(h, q).start()
                cross(h, q).start()
            if last:
                near(2 * h - 1, [q])
                if q == parts - 1:
                    for msg in messages(2 * h - 1):
                        msg.start()
                b_dev = dev(pos + reach, swap(pos, core))
                pieces = [(q, [z for z in every if z <= q])] + [(z, [q]) for z in range(q)]
                for qa, qb in pieces:
                    score(far, from_l.at[h - 1], from_r.at[h - 1], 0, b_dev, [qa], qb)
        if last:
            for msg in messages(far):
                msg.start()
        else:
            for q in range(parts):
                cross(h, q).wait_recv()
            for d in (2 * h - 1, 2 * h):
                near(d, every)
                for msg in messages(d):
                    msg.start()

    for h in range(reach):
        for q in range(parts):
            right(h, q).wait_send()
            left(h, q).wait_send()
            cross(h, q).wait_send()
    for d in range(1, far + 1):
        for msg in messages(d):
            msg.wait_send()
        for e in range(1 if d == far else CORES):
            b_msg(d, e, e).wait_recv()
        if split(d)[0] > 0:
            a_msg(d).wait_recv()

    lane = lax.broadcasted_iota(jnp.int32, (1, rows), 1)
    live = lane < 0
    for t in range(parts):
        live = live | ((lane >= t * TILE) & (lane < t * TILE + counts_ref[me * parts + t]))
    for k in range(best_ref.shape[0]):
        best_ref[k : k + 1, :] = jnp.where(live, table[wanted_ref[k]], 0.0)


def body(chips, cols, emb, wanted, counts):
    rows, width = emb.shape
    parts = rows // TILE
    reach = chips // 4
    far = 2 * reach
    data = pltpu.SemaphoreType.DMA((reach, parts))
    req = wanted.shape[0]
    smem = pl.BlockSpec(memory_space=pltpu.SMEM)
    vmem = pl.BlockSpec(memory_space=pltpu.VMEM)
    best, own = pl.pallas_call(
        functools.partial(kernel, chips, cols),
        out_shape=(
            jax.ShapeDtypeStruct((req, rows), jnp.float32),
            jax.ShapeDtypeStruct((1, rows), jnp.float32),
        ),
        in_specs=[smem, smem, vmem],
        out_specs=(vmem, vmem),
        scratch_shapes=[
            pltpu.VMEM((parts, TILE, width), jnp.bfloat16),
            pltpu.VMEM((reach, parts, TILE, width), jnp.bfloat16),
            pltpu.VMEM((reach, parts, TILE, width), jnp.bfloat16),
            pltpu.VMEM((reach, parts, TILE, width), jnp.bfloat16),
            pltpu.VMEM((chips * CORES * parts, 1, rows), jnp.float32),
            pltpu.VMEM((far, CORES * parts, 1, rows), jnp.float32),
            pltpu.VMEM((far, CORES, parts, 1, rows), jnp.float32),
            data, data, data, data, data, data,
            pltpu.SemaphoreType.DMA((far,)),
            pltpu.SemaphoreType.DMA((far,)),
            pltpu.SemaphoreType.DMA((far, CORES)),
            pltpu.SemaphoreType.DMA((far, CORES)),
        ],
        compiler_params=pltpu.CompilerParams(collective_id=0, has_side_effects=True),
    )(wanted, counts, emb)
    return best, own.reshape(rows)


def solution(mesh):
    chips = mesh.shape["clus"] // CORES
    cols = LAYER // mesh.shape["slab"]
    in_specs = (P(("slab", "clus"), None), P(("slab", "clus")), P("slab"))
    out_specs = (P(None, ("slab", "clus")), P(("slab", "clus")))
    return jax.shard_map(
        functools.partial(body, chips, cols), mesh=mesh,
        in_specs=in_specs, out_specs=out_specs, check_vma=False,
    )
```

time: 127 us -> 38.5 us (0.30)
  the two profiles are of different devices: /device:TPU:13 before, /device:TPU:0 now
where the time goes in v1:
time: 38.5 us; the launch traced here: 38.3 us
  Pallas kernels  35.7 us (93%)
  local copies, waits for them, and re-layouts  1.89 us (5%)
  between operations  0.65 us (2%)
    pallas_call x1, Pallas kernels, body(): pl.pallas_call(functools.partial(kernel, chips, cols), out_shape=(jax.Sha...  35.7 us
    unnamed x4, local copies, waits for them, and re-layouts  1.89 us

profile of v1, /device:TPU:0, one launch (start us, length us, event | category | flops | bytes accessed | tf_op | source)
XLA Modules:
  0.0 38.3 jit_solution(1237751533933672171)
XLA Ops:
  0.6 35.7 %shard_map.50 = (f32[16,256]{1,0:T(8,128)}, f32[1,256]{1,0:T(1,128)}) custom-call(s32[16]{0:T(128)} %wanted_ref.1, s32[32]{0:T(128)} %counts_ref.1, bf16[256,1024]{1,0:T(8,128)(2,1)} %emb_ref.1), custom_call_target="tpu_custom_call" | custom-call | tf_op jit(solution)/shard_map/pallas_call | solution.py:267
  36.4 0.0 copy-start
  36.4 1.3 %copy.7 = f32[16,256]{1,0:T(8,128)} copy(f32[16,256]{1,0:T(8,128)} %get-tuple-element.8) | data formatting | bytes 32768
  37.7 0.0 copy-done
  37.7 0.6 %copy.8 = f32[256]{0:T(256)} copy(f32[256]{0:T(256)S(1)} %bitcast.1) | data formatting | bytes 2048
Async XLA Ops:
  36.4 1.3 %copy-start = (f32[1,256]{1,0:T(1,128)S(1)}, f32[1,256]{1,0:T(1,128)}, u32[]{:S(2)}) copy-start(f32[1,256]{1,0:T(1,128)} %get-tuple-element.5) | copy-start | bytes 3076

commit v2 on v1

--- a/solution.py
+++ b/solution.py
@@ -31,12 +31,12 @@
 
 
 def kernel(
-    chips, cols, wanted_ref, counts_ref, emb_ref, best_ref, own_ref,
-    unit, from_l, from_r, across, table, res_a, res_b,
+    chips, cols, wanted_hbm, counts_hbm, emb_hbm, best_ref, own_ref,
+    wanted_ref, counts_ref, emb_ref, load_sem, unit, from_l, from_r, across, table, res_a, res_b,
     r_send, r_recv, l_send, l_recv, x_send, x_recv,
     a_send, a_recv, b_send, b_recv,
 ):
-    rows, width = emb_ref.shape
+    rows, width = emb_hbm.shape
     parts = rows // TILE
     reach = chips // 4
     far = 2 * reach
@@ -57,17 +57,21 @@
         return c + x * (1 - 2 * c)
 
     barrier = pltpu.get_barrier_semaphore()
+    loads = [
+        pltpu.make_async_copy(emb_hbm.at[pl.ds(q * TILE, TILE)], emb_ref.at[pl.ds(q * TILE, TILE)], load_sem.at[q])
+        for q in range(parts)
+    ]
+    loads.append(pltpu.make_async_copy(counts_hbm, counts_ref, load_sem.at[parts]))
+    loads.append(pltpu.make_async_copy(wanted_hbm, wanted_ref, load_sem.at[parts + 1]))
+    for load in loads:
+        load.start()
 
     def greet(target):
         pl.semaphore_signal(barrier, inc=1, device_id={"clus": target}, device_id_type=MESH)
 
     greet(dev(pos, other))
-    for i in range(1, reach + 1):
-        greet(dev(pos + i, core))
-    for j in range(1, reach):
-        greet(dev(pos - j, 0))
-        greet(dev(pos - j, 1))
-    greet(dev(pos - reach, swap(pos - reach, core)))
+    greet(dev(pos + 1, core))
+    greet(dev(pos - 1, core))
 
     @pl.when(crossed(pos) == 1)
     def _():
@@ -100,12 +104,15 @@
             unit[q, s : s + step, :] = (wide * lax.rsqrt(total + 1e-06)).astype(jnp.bfloat16)
 
     for q in range(parts):
+        loads[q].wait()
         normalize(q)
         if q == 0:
-            pl.semaphore_wait(barrier, 3 * reach + crossed(pos - 1))
+            pl.semaphore_wait(barrier, 3 + crossed(pos - 1))
         right(0, q).start()
         left(0, q).start()
         cross(0, q).start()
+    for load in loads[parts:]:
+        load.wait()
 
     def rows_of(ref, q):
         return ref[q]
@@ -262,7 +269,7 @@
     far = 2 * reach
     data = pltpu.SemaphoreType.DMA((reach, parts))
     req = wanted.shape[0]
-    smem = pl.BlockSpec(memory_space=pltpu.SMEM)
+    hbm = pl.BlockSpec(memory_space=pltpu.HBM)
     vmem = pl.BlockSpec(memory_space=pltpu.VMEM)
     best, own = pl.pallas_call(
         functools.partial(kernel, chips, cols),
@@ -270,9 +277,13 @@
             jax.ShapeDtypeStruct((req, rows), jnp.float32),
             jax.ShapeDtypeStruct((1, rows), jnp.float32),
         ),
-        in_specs=[smem, smem, vmem],
+        in_specs=[hbm, hbm, hbm],
         out_specs=(vmem, vmem),
         scratch_shapes=[
+            pltpu.SMEM(wanted.shape, jnp.int32),
+            pltpu.SMEM(counts.shape, jnp.int32),
+            pltpu.VMEM((rows, width), jnp.bfloat16),
+            pltpu.SemaphoreType.DMA((parts + 2,)),
             pltpu.VMEM((parts, TILE, width), jnp.bfloat16),
             pltpu.VMEM((reach, parts, TILE, width), jnp.bfloat16),
             pltpu.VMEM((reach, parts, TILE, width), jnp.bfloat16),

time: 38.5 us -> 36.9 us (0.958)
  Pallas kernels: 35.7 us -> 34.1 us
    pallas_call x1, Pallas kernels: 35.7 us -> 34.1 us  [body(): pl.pallas_call(functools.partial(kernel, chips, cols), out_shape=(jax.Sha...]
where the time goes in v2:
time: 36.9 us; the launch traced here: 36.7 us
  Pallas kernels  34.1 us (92%)
  local copies, waits for them, and re-layouts  1.89 us (5%)
  between operations  0.65 us (2%)
    pallas_call x1, Pallas kernels, body(): pl.pallas_call(functools.partial(kernel, chips, cols), out_shape=(jax.Sha...  34.1 us
    unnamed x4, local copies, waits for them, and re-layouts  1.89 us

profile of v2, /device:TPU:0, one launch (start us, length us, event | category | flops | bytes accessed | tf_op | source)
XLA Modules:
  0.0 36.7 jit_solution(10043264817719580744)
XLA Ops:
  0.6 34.1 %shard_map.50 = (f32[16,256]{1,0:T(8,128)}, f32[1,256]{1,0:T(1,128)}) custom-call(s32[16]{0:T(128)} %wanted_hbm.1, s32[32]{0:T(128)} %counts_hbm.1, bf16[256,1024]{1,0:T(8,128)(2,1)} %emb_hbm.1), custom_call_target="tpu_custom_call" | custom-call | tf_op jit(solution)/shard_map/pallas_call | solution.py:274
  34.8 0.0 copy-start
  34.8 1.3 %copy.7 = f32[16,256]{1,0:T(8,128)} copy(f32[16,256]{1,0:T(8,128)} %get-tuple-element.8) | data formatting | bytes 32768
  36.1 0.0 copy-done
  36.1 0.6 %copy.8 = f32[256]{0:T(256)} copy(f32[256]{0:T(256)S(1)} %bitcast.1) | data formatting | bytes 2048
Async XLA Ops:
  34.8 1.3 %copy-start = (f32[1,256]{1,0:T(1,128)S(1)}, f32[1,256]{1,0:T(1,128)}, u32[]{:S(2)}) copy-start(f32[1,256]{1,0:T(1,128)} %get-tuple-element.5) | copy-start | bytes 3076

commit v3 on v2

--- a/solution.py
+++ b/solution.py
@@ -139,7 +139,7 @@
         keep = (i0 < count) & (i0 != i1)
         value = jnp.max(jnp.where(keep, square, -jnp.inf), axis=0, keepdims=True)
         lane = lax.broadcasted_iota(jnp.int32, value.shape, 1)
-        own_ref[:, t * TILE : (t + 1) * TILE] = jnp.where(lane < count, value, 0.0)
+        own_ref[t * TILE : (t + 1) * TILE] = jnp.where(lane < count, value, 0.0).reshape(TILE)
 
     for q in range(parts):
         cross(0, q).wait_recv()
@@ -262,6 +262,11 @@
         best_ref[k : k + 1, :] = jnp.where(live, table[wanted_ref[k]], 0.0)
 
 
+def settle(best_in, own_in, best_out, own_out):
+    best_out[...] = best_in[...]
+    own_out[...] = own_in[...]
+
+
 def body(chips, cols, emb, wanted, counts):
     rows, width = emb.shape
     parts = rows // TILE
@@ -275,7 +280,7 @@
         functools.partial(kernel, chips, cols),
         out_shape=(
             jax.ShapeDtypeStruct((req, rows), jnp.float32),
-            jax.ShapeDtypeStruct((1, rows), jnp.float32),
+            jax.ShapeDtypeStruct((rows,), jnp.float32),
         ),
         in_specs=[hbm, hbm, hbm],
         out_specs=(vmem, vmem),
@@ -297,9 +302,18 @@
             pltpu.SemaphoreType.DMA((far, CORES)),
             pltpu.SemaphoreType.DMA((far, CORES)),
         ],
-        compiler_params=pltpu.CompilerParams(collective_id=0, has_side_effects=True),
-    )(wanted, counts, emb)
-    return best, own.reshape(rows)
+        compiler_params=pltpu.CompilerParams(collective_id=0, has_side_effects=True, vmem_limit_bytes=(3 * reach + 2) * rows * width * 2 + (8 << 20)),
+    )(*(pltpu.with_memory_space_constraint(z, pltpu.HBM) for z in (wanted, counts, emb)))
+    return pl.pallas_call(
+        settle,
+        out_shape=(
+            jax.ShapeDtypeStruct(best.shape, best.dtype),
+            jax.ShapeDtypeStruct(own.shape, own.dtype),
+        ),
+        in_specs=[vmem, vmem],
+        out_specs=(vmem, vmem),
+        compiler_params=pltpu.CompilerParams(vmem_limit_bytes=1 << 20),
+    )(best, own)
 
 
 def solution(mesh):

time: 36.9 us -> 34.9 us (0.946)
  local copies, waits for them, and re-layouts: 1.89 us -> 0 us
    unnamed x4 -> x0, local copies, waits for them, and re-layouts: 1.89 us -> none
    pallas_call x0 -> x1, Pallas kernels: none -> 0.61 us  [body(): pl.pallas_call(settle, out_shape=(jax.ShapeDtypeStruct(best.shape, best.d...]
    pallas_call x1, Pallas kernels: 34.1 us -> 33.5 us  [body(): pl.pallas_call(functools.partial(kernel, chips, cols), out_shape=(jax.Sha...]
where the time goes in v3:
time: 34.9 us; the launch traced here: 34.8 us
  Pallas kernels  34.1 us (98%)
  between operations  0.64 us (2%)
    pallas_call x1, Pallas kernels, body(): pl.pallas_call(functools.partial(kernel, chips, cols), out_shape=(jax.Sha...  33.5 us

profile of v3, /device:TPU:0, one launch (start us, length us, event | category | flops | bytes accessed | tf_op | source)
XLA Modules:
  0.0 34.8 jit_solution(4046333296992842944)
XLA Ops:
  0.6 33.5 %shard_map.50 = (f32[16,256]{1,0:T(8,128)S(1)}, f32[256]{0:T(256)S(1)}) custom-call(s32[16]{0:T(128)} %wanted_hbm.1, s32[32]{0:T(128)} %counts_hbm.1, bf16[256,1024]{1,0:T(8,128)(2,1)} %emb_hbm.1), custom_call_target="tpu_custom_call" | custom-call | tf_op jit(solution)/shard_map/pallas_call | solution.py:279
  34.2 0.6 %shard_map.51 = (f32[16,256]{1,0:T(8,128)}, f32[256]{0:T(256)}) custom-call(f32[16,256]{1,0:T(8,128)S(1)} %get-tuple-element.4.best_in, f32[256]{0:T(256)S(1)} %get-tuple-element.5.own_in), custom_call_target="tpu_custom_call" | custom-call | tf_op jit(solution)/shard_map/pallas_call | solution.py:307
